TPU v7x, 32 devices: a whole 2x2x4 slice. The times are simulated.
32 devices in a mesh: row: 8 (over y, x, core), col: 4 (over z).
Axes of the slice: x: 2, y: 2, z: 4, core: 2. Of those that a mesh axis runs over, the one named last changes fastest.
Arguments:
- dual_ops: float32 [8, 4, 2048, 2048], P('row', 'col'), as said below
- basis: float32 [8, 4, 4, 64, 512], P('row', 'col'), may hold values from -0.125 to 0.125
- coarse_inverse: float32 [2048, 2048], P('row', 'col')
- gap_rhs: float32 [8, 4, 4, 32, 512], P('row', 'col'), may hold values from -6 to 6
- coarse_rhs: float32 [8, 4, 32, 64], P('row', 'col'), may hold values from -6 to 6
- contact_mask: int32 [8, 4, 4, 512], P('row', 'col'), may hold values 0 or 1
Outputs:
- multipliers: float32 [8, 4, 4, 32, 512], P('row', 'col')
- projected_grad: float32 [8, 4, 4, 32, 512], P('row', 'col')
Inputs may be any that keep to these rules, and one draw needn't show every extreme that they name: `dual_ops`: each subdomain's dual operator is symmetric and positive definite.
All inputs are finite; a program needn't handle non-finite values. No bound on the sum of `contact_mask` on one device may be relied on, other than what follows from the above.
Results may differ from a plain program's by a relative error of at most 0.00025.
Values sent between devices are 32-bit elements; how exact they have to be, the bound alone decides.
A program may use at most 128 MiB of HBM per device.

v0:
```python
import jax
import jax.numpy as jnp
from jax import lax
from jax.sharding import PartitionSpec as P

MDEV = 64
ITERS = 6
HIGH = lax.Precision.HIGHEST


def padded(block, sides, width):
    for axis, dim in sides:
        count = lax.axis_size(axis)
        forward = [(i, i + 1) for i in range(count - 1)]
        backward = [(target, source) for source, target in forward]
        low = lax.ppermute(
            lax.slice_in_dim(block, block.shape[dim] - width, None, axis=dim), axis, forward
        )
        high = lax.ppermute(lax.slice_in_dim(block, 0, width, axis=dim), axis, backward)
        block = jnp.concatenate([low, block, high], axis=dim)
    return block


def neighbour_faces(values):
    rows_padded = padded(values[0:2], (("row", 0),), 1)
    cols_padded = padded(values[2:4], (("col", 0),), 1)
    return jnp.stack([rows_padded[0], rows_padded[3], cols_padded[0], cols_padded[3]], axis=0)


def shards(dual_ops, basis, coarse_inverse, gap_rhs, coarse_rhs, contact_mask):
    face_len = gap_rhs.shape[-1]
    blocks = dual_ops[0, 0].reshape(4, face_len, 4, face_len)
    local_basis = basis[0, 0]
    row_idx = lax.axis_index("row")
    col_idx = lax.axis_index("col")
    n_rows = lax.axis_size("row")
    n_cols = lax.axis_size("col")
    has_nb = jnp.stack([row_idx > 0, row_idx < n_rows - 1, col_idx > 0, col_idx < n_cols - 1])
    weight = jnp.where(has_nb, 0.5, 1.0).astype(jnp.float32)[:, None, None]
    contact = jnp.logical_and(contact_mask[0, 0] == 1, jnp.logical_not(has_nb)[:, None])[:, None, :]

    def apply_dual(vector):
        return jnp.einsum("gjfi,fki->gkj", blocks, vector, precision=HIGH)

    def coarse(coef):
        gathered = lax.all_gather(coef, "row", axis=1, tiled=True)
        partial_amps = lax.dot_general(
            gathered,
            coarse_inverse,
            (((1,), (1,)), ((), ())),
            precision=HIGH,
            preferred_element_type=jnp.float32,
        )
        summed = lax.psum(partial_amps, "col")
        return lax.dynamic_slice_in_dim(summed, col_idx * MDEV, MDEV, 1)

    def expand_sum(amps):
        own = jnp.einsum("fji,kj->fki", local_basis, amps, precision=HIGH)
        return own + neighbour_faces(own)

    local_rhs = gap_rhs[0, 0]
    dvec = local_rhs + neighbour_faces(local_rhs)
    multipliers = expand_sum(coarse(coarse_rhs[0, 0]))
    projected = jnp.zeros_like(multipliers)
    for step in range(ITERS):
        applied = apply_dual(multipliers)
        grad = applied + neighbour_faces(applied) - dvec
        projected = grad - expand_sum(
            coarse(jnp.einsum("fji,fki->kj", local_basis, grad, precision=HIGH))
        )
        image = apply_dual(projected)
        numer = jnp.sum(weight * grad * projected, axis=(0, 2))
        denom = jnp.sum(projected * image, axis=(0, 2))
        numer_all, denom_all = lax.psum((numer, denom), ("row", "col"))
        ratio = numer_all / denom_all
        multipliers = multipliers - ratio[None, :, None] * projected
        multipliers = jnp.where(contact, jnp.maximum(multipliers, 0.0), multipliers)
    return (multipliers[None, None], projected[None, None])


def solution(mesh):
    return jax.shard_map(
        shards,
        mesh=mesh,
        in_specs=(
            P("row", "col", None, None),
            P("row", "col", None, None, None),
            P("row", "col"),
            P("row", "col", None, None, None),
            P("row", "col", None, None),
            P("row", "col", None, None),
        ),
        out_specs=(P("row", "col", None, None, None), P("row", "col", None, None, None)),
        check_vma=False,
    )
```

profile of v0, /device:TPU:0, one launch (start us, length us, event | category | flops | bytes accessed | tf_op | source)
XLA Modules:
  0.0 938.7 jit_solution(12016818391664905516)
XLA Ops:
  1.5 10.8 %all-gather = f32[1,1,32,512]{2,1,0,3:T(1,128)S(1)} all-gather(f32[1,1,32,64]{2,1,0,3:T(1,128)S(1)} %copy.38), channel_id=2, replica_groups=mesh['row'=8,'col'=4] {'row'}, dimensions={3}, use_global_device_ids=true | all-gather | bytes 73728 | tf_op jit(solution)/shard_map/all_gather | solution.py:46
  12.3 1.6 fusion.178
  13.9 19.3 %psum.133 = f32[32,256]{1,0:T(8,128)S(1)} all-reduce(f32[32,256]{1,0:T(8,128)S(1)} %fusion.178), channel_id=1, replica_groups=mesh['row'=8,'col'=4] {'col'}, use_global_device_ids=true, to_apply=%region_0.1 | all-reduce | flops 8192 | bytes 65536 | tf_op jit(solution)/shard_map/psum | solution.py:54
  36.2 4.5 collective-permute-start.2
  43.0 4.2 collective-permute-start.8
  47.3 20.4 %reshape_squeeze.3 = f32[4,512,4,512]{3,2,1,0:T(4,128)} reshape(f32[1,1,2048,2048]{3,2,1,0:T(8,128)} %param.6) | data formatting | bytes 33554432 | tf_op jit(solution)/shard_map/reshape;squeeze | solution.py:32
  67.8 1.4 collective-permute-start.9
  70.5 4.7 collective-permute-start.10
  75.3 24.6 %fusion.24 = f32[4,32,512]{2,1,0:T(8,128)S(1)} fusion(f32[4,512,4,512]{3,2,1,0:T(4,128)} %reshape_squeeze.3, f32[4,32,512]{2,1,0:T(8,128)S(1)} %convolution_bitcast_fusion.6, f32[1,32,512]{2,1,0:T(8,128)S(1)} %collective-permute-done.3, f32[1,32,512]{2,1,0:T(8,128)S(1)} %collective-permute-done.2, f32[1,32,512]{2,1,0:T(8,128)S(1)} %collective-permute-done.1, ...), kind=kOutput, calls=%fused_computation.24 | convolution fusion | flops 1610874880 | bytes 17563648 | tf_op jit(solution)/shard_map/gjfi,fki->gkj/dot_general | solution.py:43
  99.9 3.7 collective-permute-start.4
  104.9 4.5 collective-permute-start.6
  111.4 2.5 collective-permute-done.5
  114.5 13.2 %all-gather.1 = f32[8,64,32]{1,2,0:T(8,128)S(1)} all-gather(f32[1,64,32]{1,2,0:T(8,128)S(1)} %convolution_bitcast_fusion.12), channel_id=1, replica_groups=mesh['row'=8,'col'=4] {'row'}, dimensions={0}, use_global_device_ids=true | all-gather | bytes 73728 | tf_op jit(solution)/shard_map/all_gather | solution.py:46
  128.5 16.0 %psum.134 = f32[32,256]{1,0:T(8,128)S(1)} all-reduce(f32[32,256]{1,0:T(8,128)S(1)} %fusion.179), channel_id=1, replica_groups=mesh['row'=8,'col'=4] {'col'}, use_global_device_ids=true, to_apply=%region_1.2 | all-reduce | flops 8192 | bytes 65536 | tf_op jit(solution)/shard_map/psum | solution.py:54
  147.5 4.5 collective-permute-start.14
  152.1 1.5 collective-permute-start.13
  154.0 2.5 collective-permute-done.13
  156.7 22.3 %fusion.78 = f32[32]{0:T(128)S(1)} fusion(f32[4,32,512]{2,1,0:T(8,128)S(1)} %get-tuple-element.27, f32[4,512,4,512]{3,2,1,0:T(4,128)} %reshape_squeeze.3), kind=kOutput, calls=%fused_computation.49 | convolution fusion | flops 1610743808 | bytes 17039488 | tf_op jit(solution)/shard_map/gjfi,fki->gkj/dot_general | solution.py:43
  179.0 41.7 %all-reduce.5 = (f32[32]{0:T(128)S(1)}, f32[32]{0:T(128)S(1)}) all-reduce(f32[32]{0:T(128)S(1)} %get-tuple-element.26, f32[32]{0:T(128)S(1)} %fusion.78), channel_id=1, replica_groups=mesh['row'=8,'col'=4] {'row','col'}, use_global_device_ids=true, to_apply=%region_3.4 | all-reduce | flops 64 | bytes 512 | tf_op jit(solution)/shard_map/psum | solution.py:74
  220.8 24.6 %fusion.30 = f32[4,32,512]{2,1,0:T(8,128)S(1)} fusion(f32[4,512,4,512]{3,2,1,0:T(4,128)} %reshape_squeeze.3, f32[4,32,512]{2,1,0:T(8,128)S(1)} %maximum_select_fusion.5), kind=kOutput, calls=%fused_computation.26 | convolution fusion | flops 1610612736 | bytes 17301504 | tf_op jit(solution)/shard_map/gjfi,fki->gkj/dot_general | solution.py:43
  248.0 4.5 collective-permute-start.18
  254.4 3.3 collective-permute-done.17
  258.3 11.4 %all-gather.2 = f32[8,64,32]{1,2,0:T(8,128)S(1)} all-gather(f32[1,64,32]{1,2,0:T(8,128)S(1)} %convolution_bitcast_fusion.11), channel_id=1, replica_groups=mesh['row'=8,'col'=4] {'row'}, dimensions={0}, use_global_device_ids=true | all-gather | bytes 73728 | tf_op jit(solution)/shard_map/all_gather | solution.py:46
  270.4 17.6 %psum.137 = f32[32,256]{1,0:T(8,128)S(1)} all-reduce(f32[32,256]{1,0:T(8,128)S(1)} %fusion.180), channel_id=1, replica_groups=mesh['row'=8,'col'=4] {'col'}, use_global_device_ids=true, to_apply=%region_6.7 | all-reduce | flops 8192 | bytes 65536 | tf_op jit(solution)/shard_map/psum | solution.py:54
  291.1 4.5 collective-permute-start.22
  297.6 2.5 collective-permute-done.21
  300.3 22.3 %fusion.81 = f32[32]{0:T(128)S(1)} fusion(f32[4,32,512]{2,1,0:T(8,128)S(1)} %get-tuple-element.23, f32[4,512,4,512]{3,2,1,0:T(4,128)} %reshape_squeeze.3), kind=kOutput, calls=%fused_computation.50 | convolution fusion | flops 1610743808 | bytes 17039488 | tf_op jit(solution)/shard_map/gjfi,fki->gkj/dot_general | solution.py:43
  322.6 41.5 %all-reduce.4 = (f32[32]{0:T(128)S(1)}, f32[32]{0:T(128)S(1)}) all-reduce(f32[32]{0:T(128)S(1)} %get-tuple-element.22, f32[32]{0:T(128)S(1)} %fusion.81), channel_id=1, replica_groups=mesh['row'=8,'col'=4] {'row','col'}, use_global_device_ids=true, to_apply=%region_8.9 | all-reduce | flops 64 | bytes 512 | tf_op jit(solution)/shard_map/psum | solution.py:74
  364.1 24.4 %fusion.36 = f32[4,32,512]{2,1,0:T(8,128)S(1)} fusion(f32[4,512,4,512]{3,2,1,0:T(4,128)} %reshape_squeeze.3, f32[4,32,512]{2,1,0:T(8,128)S(1)} %maximum_select_fusion.5, f32[4,32,512]{2,1,0:T(8,128)S(1)} %get-tuple-element.23, f32[32]{0:T(128)S(1)} %div.19, pred[4,512]{1,0:T(4,128)(4,1)S(1)} %bitcast_and_fusion), kind=kOutput, calls=%fused_computation.28 | convolution fusion | flops 1610874880 | bytes 17565824 | tf_op jit(solution)/shard_map/gjfi,fki->gkj/dot_general | solution.py:43
  391.1 4.5 collective-permute-start.26
  397.6 3.2 collective-permute-done.25
  401.4 11.4 %all-gather.3 = f32[8,64,32]{1,2,0:T(8,128)S(1)} all-gather(f32[1,64,32]{1,2,0:T(8,128)S(1)} %convolution_bitcast_fusion.10), channel_id=1, replica_groups=mesh['row'=8,'col'=4] {'row'}, dimensions={0}, use_global_device_ids=true | all-gather | bytes 73728 | tf_op jit(solution)/shard_map/all_gather | solution.py:46
  413.5 17.9 %psum.140 = f32[32,256]{1,0:T(8,128)S(1)} all-reduce(f32[32,256]{1,0:T(8,128)S(1)} %fusion.181), channel_id=1, replica_groups=mesh['row'=8,'col'=4] {'col'}, use_global_device_ids=true, to_apply=%region_11.12 | all-reduce | flops 8192 | bytes 65536 | tf_op jit(solution)/shard_map/psum | solution.py:54
  434.5 4.5 collective-permute-start.30
  440.9 2.5 collective-permute-done.29
  443.7 22.3 %fusion.84 = f32[32]{0:T(128)S(1)} fusion(f32[4,32,512]{2,1,0:T(8,128)S(1)} %get-tuple-element.21, f32[4,512,4,512]{3,2,1,0:T(4,128)} %reshape_squeeze.3), kind=kOutput, calls=%fused_computation.51 | convolution fusion | flops 1610743808 | bytes 17039488 | tf_op jit(solution)/shard_map/gjfi,fki->gkj/dot_general | solution.py:43
  465.9 41.4 %all-reduce.3 = (f32[32]{0:T(128)S(1)}, f32[32]{0:T(128)S(1)}) all-reduce(f32[32]{0:T(128)S(1)} %get-tuple-element.20, f32[32]{0:T(128)S(1)} %fusion.84), channel_id=1, replica_groups=mesh['row'=8,'col'=4] {'row','col'}, use_global_device_ids=true, to_apply=%region_13.14 | all-reduce | flops 64 | bytes 512 | tf_op jit(solution)/shard_map/psum | solution.py:74
  507.5 24.6 %fusion.42 = f32[4,32,512]{2,1,0:T(8,128)S(1)} fusion(f32[4,512,4,512]{3,2,1,0:T(4,128)} %reshape_squeeze.3, f32[4,32,512]{2,1,0:T(8,128)S(1)} %maximum_select_fusion.3), kind=kOutput, calls=%fused_computation.30 | convolution fusion | flops 1610612736 | bytes 17301504 | tf_op jit(solution)/shard_map/gjfi,fki->gkj/dot_general | solution.py:43
  534.7 4.5 collective-permute-start.34
  541.2 3.3 collective-permute-done.33
  545.0 11.4 %all-gather.4 = f32[8,64,32]{1,2,0:T(8,128)S(1)} all-gather(f32[1,64,32]{1,2,0:T(8,128)S(1)} %convolution_bitcast_fusion.9), channel_id=1, replica_groups=mesh['row'=8,'col'=4] {'row'}, dimensions={0}, use_global_device_ids=true | all-gather | bytes 73728 | tf_op jit(solution)/shard_map/all_gather | solution.py:46
  557.2 17.7 %psum.143 = f32[32,256]{1,0:T(8,128)S(1)} all-reduce(f32[32,256]{1,0:T(8,128)S(1)} %fusion.182), channel_id=1, replica_groups=mesh['row'=8,'col'=4] {'col'}, use_global_device_ids=true, to_apply=%region_16.17 | all-reduce | flops 8192 | bytes 65536 | tf_op jit(solution)/shard_map/psum | solution.py:54
  577.9 4.5 collective-permute-start.38
  584.4 2.5 collective-permute-done.37
  587.1 22.3 %fusion.87 = f32[32]{0:T(128)S(1)} fusion(f32[4,32,512]{2,1,0:T(8,128)S(1)} %get-tuple-element.19, f32[4,512,4,512]{3,2,1,0:T(4,128)} %reshape_squeeze.3), kind=kOutput, calls=%fused_computation.52 | convolution fusion | flops 1610743808 | bytes 17039488 | tf_op jit(solution)/shard_map/gjfi,fki->gkj/dot_general | solution.py:43
  609.4 41.7 %all-reduce.2 = (f32[32]{0:T(128)S(1)}, f32[32]{0:T(128)S(1)}) all-reduce(f32[32]{0:T(128)S(1)} %get-tuple-element.18, f32[32]{0:T(128)S(1)} %fusion.87), channel_id=1, replica_groups=mesh['row'=8,'col'=4] {'row','col'}, use_global_device_ids=true, to_apply=%region_18.19 | all-reduce | flops 64 | bytes 512 | tf_op jit(solution)/shard_map/psum | solution.py:74
  651.1 24.4 %fusion.48 = f32[4,32,512]{2,1,0:T(8,128)S(1)} fusion(f32[4,512,4,512]{3,2,1,0:T(4,128)} %reshape_squeeze.3, f32[4,32,512]{2,1,0:T(8,128)S(1)} %maximum_select_fusion.3, f32[4,32,512]{2,1,0:T(8,128)S(1)} %get-tuple-element.19, f32[32]{0:T(128)S(1)} %div.21, pred[4,512]{1,0:T(4,128)(4,1)S(1)} %bitcast_and_fusion), kind=kOutput, calls=%fused_computation.32 | convolution fusion | flops 1610874880 | bytes 17565824 | tf_op jit(solution)/shard_map/gjfi,fki->gkj/dot_general | solution.py:43
  678.1 4.5 collective-permute-start.42
  684.6 3.2 collective-permute-done.41
  688.4 11.4 %all-gather.5 = f32[8,64,32]{1,2,0:T(8,128)S(1)} all-gather(f32[1,64,32]{1,2,0:T(8,128)S(1)} %convolution_bitcast_fusion.8), channel_id=1, replica_groups=mesh['row'=8,'col'=4] {'row'}, dimensions={0}, use_global_device_ids=true | all-gather | bytes 73728 | tf_op jit(solution)/shard_map/all_gather | solution.py:46
  700.5 17.6 %psum.146 = f32[32,256]{1,0:T(8,128)S(1)} all-reduce(f32[32,256]{1,0:T(8,128)S(1)} %fusion.183), channel_id=1, replica_groups=mesh['row'=8,'col'=4] {'col'}, use_global_device_ids=true, to_apply=%region_21.22 | all-reduce | flops 8192 | bytes 65536 | tf_op jit(solution)/shard_map/psum | solution.py:54
  721.3 4.5 collective-permute-start.46
  727.7 2.5 collective-permute-done.45
  730.4 22.3 %fusion.90 = f32[32]{0:T(128)S(1)} fusion(f32[4,32,512]{2,1,0:T(8,128)S(1)} %get-tuple-element.17, f32[4,512,4,512]{3,2,1,0:T(4,128)} %reshape_squeeze.3), kind=kOutput, calls=%fused_computation.53 | convolution fusion | flops 1610743808 | bytes 17039488 | tf_op jit(solution)/shard_map/gjfi,fki->gkj/dot_general | solution.py:43
  752.7 41.5 %all-reduce.1 = (f32[32]{0:T(128)S(1)}, f32[32]{0:T(128)S(1)}) all-reduce(f32[32]{0:T(128)S(1)} %get-tuple-element.16, f32[32]{0:T(128)S(1)} %fusion.90), channel_id=1, replica_groups=mesh['row'=8,'col'=4] {'row','col'}, use_global_device_ids=true, to_apply=%region_23.24 | all-reduce | flops 64 | bytes 512 | tf_op jit(solution)/shard_map/psum | solution.py:74
  794.4 24.6 %fusion.54 = f32[4,32,512]{2,1,0:T(8,128)S(1)} fusion(f32[4,512,4,512]{3,2,1,0:T(4,128)} %reshape_squeeze.3, f32[4,32,512]{2,1,0:T(8,128)S(1)} %maximum_select_fusion.1), kind=kOutput, calls=%fused_computation.34 | convolution fusion | flops 1610612736 | bytes 17301504 | tf_op jit(solution)/shard_map/gjfi,fki->gkj/dot_general | solution.py:43
  821.5 4.5 collective-permute-start.50
  828.0 3.3 collective-permute-done.49
  831.9 11.4 %all-gather.6 = f32[8,64,32]{1,2,0:T(8,128)S(1)} all-gather(f32[1,64,32]{1,2,0:T(8,128)S(1)} %convolution_bitcast_fusion.7), channel_id=1, replica_groups=mesh['row'=8,'col'=4] {'row'}, dimensions={0}, use_global_device_ids=true | all-gather | bytes 73728 | tf_op jit(solution)/shard_map/all_gather | solution.py:46
  844.0 17.7 %psum.149 = f32[32,256]{1,0:T(8,128)S(1)} all-reduce(f32[32,256]{1,0:T(8,128)S(1)} %fusion.184), channel_id=1, replica_groups=mesh['row'=8,'col'=4] {'col'}, use_global_device_ids=true, to_apply=%region_26.27 | all-reduce | flops 8192 | bytes 65536 | tf_op jit(solution)/shard_map/psum | solution.py:54
  864.8 4.5 collective-permute-start.54
  871.2 2.5 collective-permute-done.53
  874.0 22.4 %fusion.93 = f32[32]{0:T(128)S(1)} fusion(f32[4,32,512]{2,1,0:T(8,128)S(1)} %get-tuple-element.15, f32[4,512,4,512]{3,2,1,0:T(4,128)} %reshape_squeeze.3), kind=kOutput, calls=%fused_computation.54 | convolution fusion | flops 1610743808 | bytes 17039488 | tf_op jit(solution)/shard_map/gjfi,fki->gkj/dot_general | solution.py:43
  896.4 41.3 %all-reduce = (f32[32]{0:T(128)S(1)}, f32[32]{0:T(128)S(1)}) all-reduce(f32[32]{0:T(128)S(1)} %get-tuple-element.14, f32[32]{0:T(128)S(1)} %fusion.93), channel_id=1, replica_groups=mesh['row'=8,'col'=4] {'row','col'}, use_global_device_ids=true, to_apply=%region_28.29 | all-reduce | flops 64 | bytes 512 | tf_op jit(solution)/shard_map/psum | solution.py:74
  (163 shorter events, 71.5 us)
Async XLA Ops:
  0.6 32.5 %copy-start = (f32[1,1,4,64,512]{4,3,2,1,0:T(8,128)S(1)}, f32[1,1,4,64,512]{4,3,2,1,0:T(8,128)}, u32[]{:S(2)}) copy-start(f32[1,1,4,64,512]{4,3,2,1,0:T(8,128)} %param.7) | copy-start | bytes 1572868
  33.6 34.2 %collective-permute-start = (f32[1,32,512]{2,1,0:T(8,128)S(1)}, f32[1,32,512]{2,1,0:T(8,128)S(1)}, u32[]{:S(2)}, u32[]{:S(2)}) collective-permute-start(f32[1,32,512]{2,1,0:T(8,128)S(1)} %get-tuple-element.82), channel_id=1, source_target_pairs={{0,4},{4,8},{8,12},{12,16},{16,20},{20,24},{24,28},{1,5},{5,9},{9,... | collective-permute-start | bytes 196616 | tf_op jit(solution)/shard_map/ppermute | solution.py:16
  34.9 34.3 %collective-permute-start.3 = (f32[1,32,512]{2,1,0:T(8,128)S(1)}, f32[1,32,512]{2,1,0:T(8,128)S(1)}, u32[]{:S(2)}, u32[]{:S(2)}) collective-permute-start(f32[1,32,512]{2,1,0:T(8,128)S(1)} %get-tuple-element.83), channel_id=1, source_target_pairs={{1,0},{2,1},{3,2},{5,4},{6,5},{7,6},{9,8},{10,9},{11,10},{13,12},{... | collective-permute-start | bytes 196616 | tf_op jit(solution)/shard_map/ppermute | solution.py:19
  36.2 34.3 %collective-permute-start.2 = (f32[1,32,512]{2,1,0:T(8,128)S(1)}, f32[1,32,512]{2,1,0:T(8,128)S(1)}, u32[]{:S(2)}, u32[]{:S(2)}) collective-permute-start(f32[1,32,512]{2,1,0:T(8,128)S(1)} %get-tuple-element.84), channel_id=1, source_target_pairs={{0,1},{1,2},{2,3},{4,5},{5,6},{6,7},{8,9},{9,10},{10,11},{12,13},{... | collective-permute-start | bytes 196616 | tf_op jit(solution)/shard_map/ppermute | solution.py:16
  40.8 34.5 %collective-permute-start.1 = (f32[1,32,512]{2,1,0:T(8,128)S(1)}, f32[1,32,512]{2,1,0:T(8,128)S(1)}, u32[]{:S(2)}, u32[]{:S(2)}) collective-permute-start(f32[1,32,512]{2,1,0:T(8,128)S(1)} %get-tuple-element.85), channel_id=1, source_target_pairs={{4,0},{8,4},{12,8},{16,12},{20,16},{24,20},{28,24},{5,1},{9,5},{13... | collective-permute-start | bytes 196616 | tf_op jit(solution)/shard_map/ppermute | solution.py:19
  43.0 60.6 %collective-permute-start.8 = (f32[1,32,512]{2,1,0:T(8,128)S(1)}, f32[1,32,512]{2,1,0:T(8,128)S(1)}, u32[]{:S(2)}, u32[]{:S(2)}) collective-permute-start(f32[1,32,512]{2,1,0:T(8,128)S(1)} %get-tuple-element.74), channel_id=1, source_target_pairs={{0,4},{4,8},{8,12},{12,16},{16,20},{20,24},{24,28},{1,5},{5,9},{9,... | collective-permute-start | bytes 196616 | tf_op jit(solution)/shard_map/ppermute | solution.py:16
  67.7 43.1 %copy-start.4 = (s32[1,1,4,512]{3,2,1,0:T(4,128)S(1)}, s32[1,1,4,512]{3,2,1,0:T(4,128)}, u32[]{:S(2)}) copy-start(s32[1,1,4,512]{3,2,1,0:T(4,128)} %param.11) | copy-start | bytes 24580
  67.7 46.2 %copy-start.3 = (f32[1,1,4,32,512]{4,3,2,1,0:T(8,128)S(1)}, f32[1,1,4,32,512]{4,3,2,1,0:T(8,128)}, u32[]{:S(2)}) copy-start(f32[1,1,4,32,512]{4,3,2,1,0:T(8,128)} %param.9) | copy-start | bytes 786436
  67.7 60.2 %copy-start.1 = (f32[256,512]{1,0:T(8,128)S(1)}, f32[256,512]{1,0:T(8,128)}, u32[]{:S(2)}) copy-start(f32[256,512]{1,0:T(8,128)} %param.8) | copy-start | bytes 1572868
  67.8 37.1 %collective-permute-start.9 = (f32[1,32,512]{2,1,0:T(8,128)S(1)}, f32[1,32,512]{2,1,0:T(8,128)S(1)}, u32[]{:S(2)}, u32[]{:S(2)}) collective-permute-start(f32[1,32,512]{2,1,0:T(8,128)S(1)} %get-tuple-element.75), channel_id=1, source_target_pairs={{4,0},{8,4},{12,8},{16,12},{20,16},{24,20},{28,24},{5,1},{9,5},{13... | collective-permute-start | bytes 196616 | tf_op jit(solution)/shard_map/ppermute | solution.py:19
  69.2 40.3 %collective-permute-start.11 = (f32[1,32,512]{2,1,0:T(8,128)S(1)}, f32[1,32,512]{2,1,0:T(8,128)S(1)}, u32[]{:S(2)}, u32[]{:S(2)}) collective-permute-start(f32[1,32,512]{2,1,0:T(8,128)S(1)} %get-tuple-element.76), channel_id=1, source_target_pairs={{1,0},{2,1},{3,2},{5,4},{6,5},{7,6},{9,8},{10,9},{11,10},{13,12},{... | collective-permute-start | bytes 196616 | tf_op jit(solution)/shard_map/ppermute | solution.py:19
  70.5 40.4 %collective-permute-start.10 = (f32[1,32,512]{2,1,0:T(8,128)S(1)}, f32[1,32,512]{2,1,0:T(8,128)S(1)}, u32[]{:S(2)}, u32[]{:S(2)}) collective-permute-start(f32[1,32,512]{2,1,0:T(8,128)S(1)} %get-tuple-element.77), channel_id=1, source_target_pairs={{0,1},{1,2},{2,3},{4,5},{5,6},{6,7},{8,9},{9,10},{10,11},{12,13},{... | collective-permute-start | bytes 196616 | tf_op jit(solution)/shard_map/ppermute | solution.py:16
  99.9 11.0 %collective-permute-start.4 = (f32[1,32,512]{2,1,0:T(8,128)S(1)}, f32[1,32,512]{2,1,0:T(8,128)S(1)}, u32[]{:S(2)}, u32[]{:S(2)}) collective-permute-start(f32[1,32,512]{2,1,0:T(8,128)S(1)} %get-tuple-element.78), channel_id=1, source_target_pairs={{0,4},{4,8},{8,12},{12,16},{16,20},{20,24},{24,28},{1,5},{5,9},{9,... | collective-permute-start | bytes 196616 | tf_op jit(solution)/shard_map/ppermute | solution.py:16
  103.6 7.3 collective-permute-start.7
  104.9 6.4 collective-permute-start.6
  109.5 4.4 collective-permute-start.5
  144.9 8.7 collective-permute-start.12
  146.2 7.4 collective-permute-start.15
  147.5 6.4 collective-permute-start.14
  152.1 4.4 collective-permute-start.13
  245.4 8.5 collective-permute-start.16
  246.7 7.2 collective-permute-start.19
  248.0 6.4 collective-permute-start.18
  252.5 5.1 collective-permute-start.17
  288.5 8.5 collective-permute-start.20
  289.8 7.2 collective-permute-start.23
  291.1 6.4 collective-permute-start.22
  295.7 4.4 collective-permute-start.21
  388.5 8.5 collective-permute-start.24
  389.8 7.2 collective-permute-start.27
  391.1 6.4 collective-permute-start.26
  395.7 5.1 collective-permute-start.25
  431.9 8.5 collective-permute-start.28
  433.2 7.2 collective-permute-start.31
  434.5 6.4 collective-permute-start.30
  439.0 4.4 collective-permute-start.29
  532.1 8.5 collective-permute-start.32
  533.4 7.2 collective-permute-start.35
  534.7 6.4 collective-permute-start.34
  539.3 5.1 collective-permute-start.33
  575.3 8.5 collective-permute-start.36
  576.6 7.2 collective-permute-start.39
  577.9 6.4 collective-permute-start.38
  582.5 4.4 collective-permute-start.37
  675.5 8.5 collective-permute-start.40
  676.8 7.2 collective-permute-start.43
  678.1 6.4 collective-permute-start.42
  682.7 5.1 collective-permute-start.41
  718.7 8.5 collective-permute-start.44
  720.0 7.2 collective-permute-start.47
  721.3 6.4 collective-permute-start.46
  725.8 4.4 collective-permute-start.45
  818.9 8.5 collective-permute-start.48
  820.2 7.2 collective-permute-start.51
  821.5 6.4 collective-permute-start.50
  826.1 5.2 collective-permute-start.49
  862.2 8.5 collective-permute-start.52
  863.5 7.2 collective-permute-start.55
  864.8 6.4 collective-permute-start.54
  869.4 4.4 collective-permute-start.53
  874.0 64.5 %copy-start.2 = (f32[4,32,512]{2,1,0:T(8,128)}, f32[4,32,512]{2,1,0:T(8,128)S(1)}, u32[]{:S(2)}) copy-start(f32[4,32,512]{2,1,0:T(8,128)S(1)} %get-tuple-element.15) | copy-start | bytes 786436
where the time goes:
time: 944 us; the launch traced here: 939 us
  blocking collectives  454 us (48%)
  matrix products  292 us (31%)
  starting transfers between devices  124 us (13%)
  waiting for transfers between devices  40.5 us (4%)
  local copies, waits for them, and re-layouts  23.6 us (2%)
    dot_general x12, matrix products, apply_dual(): return jnp.einsum('gjfi,fki->gkj', blocks, vector, precision=HIGH)  281 us
    psum x6, blocking collectives, shards(): numer_all, denom_all = lax.psum((numer, denom), ('row', 'col'))  249 us
    psum x7, blocking collectives, coarse(): summed = lax.psum(partial_amps, 'col')  124 us
    ppermute x28, starting transfers between devices, padded(): lax.ppermute(lax.slice_in_dim(block, block.shape[dim] - width, None, axis...  87.3 us
    all_gather x7, blocking collectives, coarse(): gathered = lax.all_gather(coef, 'row', axis=1, tiled=True)  80.8 us
    ppermute x28, starting transfers between devices, padded(): lax.ppermute(lax.slice_in_dim(block, 0, width, axis=dim), axis, backward)  36.5 us
    ppermute x28, waiting for transfers between devices, padded(): lax.ppermute(lax.slice_in_dim(block, 0, width, axis=dim), axis, backward)  34 us
    another operation x1, local copies, waits for them, and re-layouts, shards(): blocks = dual_ops[0, 0].reshape(4, face_len, 4, face_len)  20.4 us
  transfers between devices with their start and end apart: 56, of which 24 were waited for; matrix products, arithmetic and copies ran while one was open for 5% of the time, Pallas kernels for 0%

commit v1 on v0

--- a/solution.py
+++ b/solution.py
@@ -43,7 +43,15 @@
         return jnp.einsum("gjfi,fki->gkj", blocks, vector, precision=HIGH)
 
     def coarse(coef):
-        gathered = lax.all_gather(coef, "row", axis=1, tiled=True)
+        ways, here = (lax.axis_size("row"), lax.axis_index("row"))
+        grown, reach = (coef, 1)
+        while reach < ways:
+            theirs = lax.ppermute(grown, "row", [(d, d ^ reach) for d in range(ways)])
+            mine_first = jnp.concatenate([grown, theirs], axis=1)
+            theirs_first = jnp.concatenate([theirs, grown], axis=1)
+            grown = jnp.where(here & reach == 0, mine_first, theirs_first)
+            reach = 2 * reach
+        gathered = grown
         partial_amps = lax.dot_general(
             gathered,
             coarse_inverse,

time: 944 us -> 945 us (level)
  blocking collectives: 454 us -> 364 us
  starting transfers between devices: 124 us -> 169 us
  waiting for transfers between devices: 40.5 us -> 80.9 us
    all_gather x7 -> x0, blocking collectives: 80.8 us -> none  [coarse(): gathered = lax.all_gather(coef, 'row', axis=1, tiled=True)]
    ppermute x0 -> x21, starting transfers between devices: none -> 43.9 us  [coarse(): theirs = lax.ppermute(grown, 'row', [(d, d ^ reach) for d in range(ways)])]
    ppermute x0 -> x21, waiting for transfers between devices: none -> 38.8 us  [coarse(): theirs = lax.ppermute(grown, 'row', [(d, d ^ reach) for d in range(ways)])]
  transfers between devices with their start and end apart: 56 -> 77, of which waited for: 24 -> 45; matrix products, arithmetic and copies ran while one was open for 5% -> 5% of each run, Pallas kernels for 0% -> 0%
where the time goes in v1:
time: 945 us; the launch traced here: 934 us
  blocking collectives  364 us (39%)
  matrix products  292 us (31%)
  starting transfers between devices  169 us (18%)
  waiting for transfers between devices  80.9 us (9%)
  local copies, waits for them, and re-layouts  21.6 us (2%)
    dot_general x12, matrix products, apply_dual(): return jnp.einsum('gjfi,fki->gkj', blocks, vector, precision=HIGH)  281 us
    psum x6, blocking collectives, shards(): numer_all, denom_all = lax.psum((numer, denom), ('row', 'col'))  241 us
    psum x7, blocking collectives, coarse(): summed = lax.psum(partial_amps, 'col')  123 us
    ppermute x28, starting transfers between devices, padded(): lax.ppermute(lax.slice_in_dim(block, block.shape[dim] - width, None, axis...  87.1 us
    ppermute x21, starting transfers between devices, coarse(): theirs = lax.ppermute(grown, 'row', [(d, d ^ reach) for d in range(ways)])  43.9 us
    ppermute x21, waiting for transfers between devices, coarse(): theirs = lax.ppermute(grown, 'row', [(d, d ^ reach) for d in range(ways)])  38.8 us
    ppermute x28, starting transfers between devices, padded(): lax.ppermute(lax.slice_in_dim(block, 0, width, axis=dim), axis, backward)  37.7 us
    ppermute x28, waiting for transfers between devices, padded(): lax.ppermute(lax.slice_in_dim(block, 0, width, axis=dim), axis, backward)  36.7 us
  transfers between devices with their start and end apart: 77, of which 45 were waited for; matrix products, arithmetic and copies ran while one was open for 5% of the time, Pallas kernels for 0%

profile of v1, /device:TPU:0, one launch (start us, length us, event | category | flops | bytes accessed | tf_op | source)
XLA Modules:
  0.0 933.9 jit_solution(1080999307292843878)
XLA Ops:
  13.2 19.8 %psum.133 = f32[32,256]{1,0:T(8,128)S(1)} all-reduce(f32[32,256]{1,0:T(8,128)S(1)} %fusion.134), channel_id=1, replica_groups=mesh['row'=8,'col'=4] {'col'}, use_global_device_ids=true, to_apply=%region_0.1 | all-reduce | flops 8192 | bytes 65536 | tf_op jit(solution)/shard_map/psum | solution.py:62
  36.1 4.5 collective-permute-start.5
  42.9 4.2 collective-permute-start.11
  47.1 20.4 %reshape_squeeze.3 = f32[4,512,4,512]{3,2,1,0:T(4,128)} reshape(f32[1,1,2048,2048]{3,2,1,0:T(8,128)} %param.6) | data formatting | bytes 33554432 | tf_op jit(solution)/shard_map/reshape;squeeze | solution.py:32
  70.3 4.5 collective-permute-start.13
  74.8 24.6 %fusion.24 = f32[4,32,512]{2,1,0:T(8,128)S(1)} fusion(f32[4,512,4,512]{3,2,1,0:T(4,128)} %reshape_squeeze.3, f32[4,32,512]{2,1,0:T(8,128)S(1)} %convolution_bitcast_fusion.6, f32[1,32,512]{2,1,0:T(8,128)S(1)} %collective-permute-done.6, f32[1,32,512]{2,1,0:T(8,128)S(1)} %collective-permute-done.5, f32[1,32,512]{2,1,0:T(8,128)S(1)} %collective-permute-done.4, ...), kind=kOutput, calls=%fused_computation.24 | convolution fusion | flops 1610874880 | bytes 17563648 | tf_op jit(solution)/shard_map/gjfi,fki->gkj/dot_general | solution.py:43
  99.5 3.7 collective-permute-start.7
  104.5 4.5 collective-permute-start.9
  114.1 3.0 collective-permute-start.15
  118.0 4.2 collective-permute-start.16
  124.8 3.1 collective-permute-done.17
  128.4 15.9 %psum.134 = f32[32,256]{1,0:T(8,128)S(1)} all-reduce(f32[32,256]{1,0:T(8,128)S(1)} %fusion.140), channel_id=1, replica_groups=mesh['row'=8,'col'=4] {'col'}, use_global_device_ids=true, to_apply=%region_1.2 | all-reduce | flops 8192 | bytes 65536 | tf_op jit(solution)/shard_map/psum | solution.py:62
  147.4 4.5 collective-permute-start.20
  157.0 22.3 %fusion.78 = f32[32]{0:T(128)S(1)} fusion(f32[4,32,512]{2,1,0:T(8,128)S(1)} %get-tuple-element.27, f32[4,512,4,512]{3,2,1,0:T(4,128)} %reshape_squeeze.3), kind=kOutput, calls=%fused_computation.49 | convolution fusion | flops 1610743808 | bytes 17039488 | tf_op jit(solution)/shard_map/gjfi,fki->gkj/dot_general | solution.py:43
  179.3 40.4 %all-reduce.5 = (f32[32]{0:T(128)S(1)}, f32[32]{0:T(128)S(1)}) all-reduce(f32[32]{0:T(128)S(1)} %get-tuple-element.26, f32[32]{0:T(128)S(1)} %fusion.78), channel_id=1, replica_groups=mesh['row'=8,'col'=4] {'row','col'}, use_global_device_ids=true, to_apply=%region_3.4 | all-reduce | flops 64 | bytes 512 | tf_op jit(solution)/shard_map/psum | solution.py:82
  219.8 24.6 %fusion.30 = f32[4,32,512]{2,1,0:T(8,128)S(1)} fusion(f32[4,512,4,512]{3,2,1,0:T(4,128)} %reshape_squeeze.3, f32[4,32,512]{2,1,0:T(8,128)S(1)} %maximum_select_fusion.5), kind=kOutput, calls=%fused_computation.26 | convolution fusion | flops 1610612736 | bytes 17301504 | tf_op jit(solution)/shard_map/gjfi,fki->gkj/dot_general | solution.py:43
  247.0 4.5 collective-permute-start.24
  253.5 3.3 collective-permute-done.23
  257.4 3.0 collective-permute-start.26
  266.1 3.2 collective-permute-done.28
  269.9 17.4 %psum.137 = f32[32,256]{1,0:T(8,128)S(1)} all-reduce(f32[32,256]{1,0:T(8,128)S(1)} %fusion.146), channel_id=1, replica_groups=mesh['row'=8,'col'=4] {'col'}, use_global_device_ids=true, to_apply=%region_6.7 | all-reduce | flops 8192 | bytes 65536 | tf_op jit(solution)/shard_map/psum | solution.py:62
  290.3 4.5 collective-permute-start.31
  296.8 3.0 collective-permute-done.30
  299.9 22.3 %fusion.81 = f32[32]{0:T(128)S(1)} fusion(f32[4,32,512]{2,1,0:T(8,128)S(1)} %get-tuple-element.23, f32[4,512,4,512]{3,2,1,0:T(4,128)} %reshape_squeeze.3), kind=kOutput, calls=%fused_computation.50 | convolution fusion | flops 1610743808 | bytes 17039488 | tf_op jit(solution)/shard_map/gjfi,fki->gkj/dot_general | solution.py:43
  322.2 40.2 %all-reduce.4 = (f32[32]{0:T(128)S(1)}, f32[32]{0:T(128)S(1)}) all-reduce(f32[32]{0:T(128)S(1)} %get-tuple-element.22, f32[32]{0:T(128)S(1)} %fusion.81), channel_id=1, replica_groups=mesh['row'=8,'col'=4] {'row','col'}, use_global_device_ids=true, to_apply=%region_8.9 | all-reduce | flops 64 | bytes 512 | tf_op jit(solution)/shard_map/psum | solution.py:82
  362.4 24.4 %fusion.36 = f32[4,32,512]{2,1,0:T(8,128)S(1)} fusion(f32[4,512,4,512]{3,2,1,0:T(4,128)} %reshape_squeeze.3, f32[4,32,512]{2,1,0:T(8,128)S(1)} %maximum_select_fusion.5, f32[4,32,512]{2,1,0:T(8,128)S(1)} %get-tuple-element.23, f32[32]{0:T(128)S(1)} %div.19, pred[4,512]{1,0:T(4,128)(4,1)S(1)} %bitcast_and_fusion), kind=kOutput, calls=%fused_computation.28 | convolution fusion | flops 1610874880 | bytes 17565824 | tf_op jit(solution)/shard_map/gjfi,fki->gkj/dot_general | solution.py:43
  389.4 4.5 collective-permute-start.35
  395.9 3.3 collective-permute-done.34
  399.8 3.0 collective-permute-start.37
  408.5 3.2 collective-permute-done.39
  412.3 17.4 %psum.140 = f32[32,256]{1,0:T(8,128)S(1)} all-reduce(f32[32,256]{1,0:T(8,128)S(1)} %fusion.152), channel_id=1, replica_groups=mesh['row'=8,'col'=4] {'col'}, use_global_device_ids=true, to_apply=%region_11.12 | all-reduce | flops 8192 | bytes 65536 | tf_op jit(solution)/shard_map/psum | solution.py:62
  432.7 4.5 collective-permute-start.42
  442.3 22.3 %fusion.84 = f32[32]{0:T(128)S(1)} fusion(f32[4,32,512]{2,1,0:T(8,128)S(1)} %get-tuple-element.21, f32[4,512,4,512]{3,2,1,0:T(4,128)} %reshape_squeeze.3), kind=kOutput, calls=%fused_computation.51 | convolution fusion | flops 1610743808 | bytes 17039488 | tf_op jit(solution)/shard_map/gjfi,fki->gkj/dot_general | solution.py:43
  464.6 40.1 %all-reduce.3 = (f32[32]{0:T(128)S(1)}, f32[32]{0:T(128)S(1)}) all-reduce(f32[32]{0:T(128)S(1)} %get-tuple-element.20, f32[32]{0:T(128)S(1)} %fusion.84), channel_id=1, replica_groups=mesh['row'=8,'col'=4] {'row','col'}, use_global_device_ids=true, to_apply=%region_13.14 | all-reduce | flops 64 | bytes 512 | tf_op jit(solution)/shard_map/psum | solution.py:82
  504.9 24.6 %fusion.42 = f32[4,32,512]{2,1,0:T(8,128)S(1)} fusion(f32[4,512,4,512]{3,2,1,0:T(4,128)} %reshape_squeeze.3, f32[4,32,512]{2,1,0:T(8,128)S(1)} %maximum_select_fusion.3), kind=kOutput, calls=%fused_computation.30 | convolution fusion | flops 1610612736 | bytes 17301504 | tf_op jit(solution)/shard_map/gjfi,fki->gkj/dot_general | solution.py:43
  532.1 4.5 collective-permute-start.46
  538.5 3.3 collective-permute-done.45
  542.4 3.0 collective-permute-start.48
  551.2 3.2 collective-permute-done.50
  554.9 17.4 %psum.143 = f32[32,256]{1,0:T(8,128)S(1)} all-reduce(f32[32,256]{1,0:T(8,128)S(1)} %fusion.158), channel_id=1, replica_groups=mesh['row'=8,'col'=4] {'col'}, use_global_device_ids=true, to_apply=%region_16.17 | all-reduce | flops 8192 | bytes 65536 | tf_op jit(solution)/shard_map/psum | solution.py:62
  575.4 4.5 collective-permute-start.53
  581.9 3.0 collective-permute-done.52
  585.0 22.3 %fusion.87 = f32[32]{0:T(128)S(1)} fusion(f32[4,32,512]{2,1,0:T(8,128)S(1)} %get-tuple-element.19, f32[4,512,4,512]{3,2,1,0:T(4,128)} %reshape_squeeze.3), kind=kOutput, calls=%fused_computation.52 | convolution fusion | flops 1610743808 | bytes 17039488 | tf_op jit(solution)/shard_map/gjfi,fki->gkj/dot_general | solution.py:43
  607.3 40.4 %all-reduce.2 = (f32[32]{0:T(128)S(1)}, f32[32]{0:T(128)S(1)}) all-reduce(f32[32]{0:T(128)S(1)} %get-tuple-element.18, f32[32]{0:T(128)S(1)} %fusion.87), channel_id=1, replica_groups=mesh['row'=8,'col'=4] {'row','col'}, use_global_device_ids=true, to_apply=%region_18.19 | all-reduce | flops 64 | bytes 512 | tf_op jit(solution)/shard_map/psum | solution.py:82
  647.7 24.4 %fusion.48 = f32[4,32,512]{2,1,0:T(8,128)S(1)} fusion(f32[4,512,4,512]{3,2,1,0:T(4,128)} %reshape_squeeze.3, f32[4,32,512]{2,1,0:T(8,128)S(1)} %maximum_select_fusion.3, f32[4,32,512]{2,1,0:T(8,128)S(1)} %get-tuple-element.19, f32[32]{0:T(128)S(1)} %div.21, pred[4,512]{1,0:T(4,128)(4,1)S(1)} %bitcast_and_fusion), kind=kOutput, calls=%fused_computation.32 | convolution fusion | flops 1610874880 | bytes 17565824 | tf_op jit(solution)/shard_map/gjfi,fki->gkj/dot_general | solution.py:43
  674.7 4.5 collective-permute-start.57
  681.2 3.3 collective-permute-done.56
  685.1 3.0 collective-permute-start.59
  693.8 3.2 collective-permute-done.61
  697.6 17.4 %psum.146 = f32[32,256]{1,0:T(8,128)S(1)} all-reduce(f32[32,256]{1,0:T(8,128)S(1)} %fusion.164), channel_id=1, replica_groups=mesh['row'=8,'col'=4] {'col'}, use_global_device_ids=true, to_apply=%region_21.22 | all-reduce | flops 8192 | bytes 65536 | tf_op jit(solution)/shard_map/psum | solution.py:62
  718.0 4.5 collective-permute-start.64
  724.5 3.0 collective-permute-done.63
  727.6 22.3 %fusion.90 = f32[32]{0:T(128)S(1)} fusion(f32[4,32,512]{2,1,0:T(8,128)S(1)} %get-tuple-element.17, f32[4,512,4,512]{3,2,1,0:T(4,128)} %reshape_squeeze.3), kind=kOutput, calls=%fused_computation.53 | convolution fusion | flops 1610743808 | bytes 17039488 | tf_op jit(solution)/shard_map/gjfi,fki->gkj/dot_general | solution.py:43
  749.9 40.2 %all-reduce.1 = (f32[32]{0:T(128)S(1)}, f32[32]{0:T(128)S(1)}) all-reduce(f32[32]{0:T(128)S(1)} %get-tuple-element.16, f32[32]{0:T(128)S(1)} %fusion.90), channel_id=1, replica_groups=mesh['row'=8,'col'=4] {'row','col'}, use_global_device_ids=true, to_apply=%region_23.24 | all-reduce | flops 64 | bytes 512 | tf_op jit(solution)/shard_map/psum | solution.py:82
  790.2 24.6 %fusion.54 = f32[4,32,512]{2,1,0:T(8,128)S(1)} fusion(f32[4,512,4,512]{3,2,1,0:T(4,128)} %reshape_squeeze.3, f32[4,32,512]{2,1,0:T(8,128)S(1)} %maximum_select_fusion.1), kind=kOutput, calls=%fused_computation.34 | convolution fusion | flops 1610612736 | bytes 17301504 | tf_op jit(solution)/shard_map/gjfi,fki->gkj/dot_general | solution.py:43
  817.4 4.5 collective-permute-start.68
  823.9 3.3 collective-permute-done.67
  827.8 3.0 collective-permute-start.70
  836.5 3.2 collective-permute-done.72
  840.3 17.4 %psum.149 = f32[32,256]{1,0:T(8,128)S(1)} all-reduce(f32[32,256]{1,0:T(8,128)S(1)} %fusion.170), channel_id=1, replica_groups=mesh['row'=8,'col'=4] {'col'}, use_global_device_ids=true, to_apply=%region_26.27 | all-reduce | flops 8192 | bytes 65536 | tf_op jit(solution)/shard_map/psum | solution.py:62
  860.7 4.5 collective-permute-start.75
  867.2 3.0 collective-permute-done.74
  870.3 22.4 %fusion.93 = f32[32]{0:T(128)S(1)} fusion(f32[4,32,512]{2,1,0:T(8,128)S(1)} %get-tuple-element.15, f32[4,512,4,512]{3,2,1,0:T(4,128)} %reshape_squeeze.3), kind=kOutput, calls=%fused_computation.54 | convolution fusion | flops 1610743808 | bytes 17039488 | tf_op jit(solution)/shard_map/gjfi,fki->gkj/dot_general | solution.py:43
  892.7 39.9 %all-reduce = (f32[32]{0:T(128)S(1)}, f32[32]{0:T(128)S(1)}) all-reduce(f32[32]{0:T(128)S(1)} %get-tuple-element.14, f32[32]{0:T(128)S(1)} %fusion.93), channel_id=1, replica_groups=mesh['row'=8,'col'=4] {'row','col'}, use_global_device_ids=true, to_apply=%region_28.29 | all-reduce | flops 64 | bytes 512 | tf_op jit(solution)/shard_map/psum | solution.py:82
  (199 shorter events, 125.6 us)
Async XLA Ops:
  3.1 4.5 collective-permute-start.1
  7.7 3.9 collective-permute-start.2
  33.5 34.0 %collective-permute-start.3 = (f32[1,32,512]{2,1,0:T(8,128)S(1)}, f32[1,32,512]{2,1,0:T(8,128)S(1)}, u32[]{:S(2)}, u32[]{:S(2)}) collective-permute-start(f32[1,32,512]{2,1,0:T(8,128)S(1)} %get-tuple-element.82), channel_id=1, source_target_pairs={{0,4},{4,8},{8,12},{12,16},{16,20},{20,24},{24,28},{1,5},{5,9},{9,... | collective-permute-start | bytes 196616 | tf_op jit(solution)/shard_map/ppermute | solution.py:16
  34.8 34.2 %collective-permute-start.6 = (f32[1,32,512]{2,1,0:T(8,128)S(1)}, f32[1,32,512]{2,1,0:T(8,128)S(1)}, u32[]{:S(2)}, u32[]{:S(2)}) collective-permute-start(f32[1,32,512]{2,1,0:T(8,128)S(1)} %get-tuple-element.83), channel_id=1, source_target_pairs={{1,0},{2,1},{3,2},{5,4},{6,5},{7,6},{9,8},{10,9},{11,10},{13,12},{... | collective-permute-start | bytes 196616 | tf_op jit(solution)/shard_map/ppermute | solution.py:19
  36.1 34.2 %collective-permute-start.5 = (f32[1,32,512]{2,1,0:T(8,128)S(1)}, f32[1,32,512]{2,1,0:T(8,128)S(1)}, u32[]{:S(2)}, u32[]{:S(2)}) collective-permute-start(f32[1,32,512]{2,1,0:T(8,128)S(1)} %get-tuple-element.84), channel_id=1, source_target_pairs={{0,1},{1,2},{2,3},{4,5},{5,6},{6,7},{8,9},{9,10},{10,11},{12,13},{... | collective-permute-start | bytes 196616 | tf_op jit(solution)/shard_map/ppermute | solution.py:16
  40.6 34.2 %collective-permute-start.4 = (f32[1,32,512]{2,1,0:T(8,128)S(1)}, f32[1,32,512]{2,1,0:T(8,128)S(1)}, u32[]{:S(2)}, u32[]{:S(2)}) collective-permute-start(f32[1,32,512]{2,1,0:T(8,128)S(1)} %get-tuple-element.85), channel_id=1, source_target_pairs={{4,0},{8,4},{12,8},{16,12},{20,16},{24,20},{28,24},{5,1},{9,5},{13... | collective-permute-start | bytes 196616 | tf_op jit(solution)/shard_map/ppermute | solution.py:19
  42.9 60.3 %collective-permute-start.11 = (f32[1,32,512]{2,1,0:T(8,128)S(1)}, f32[1,32,512]{2,1,0:T(8,128)S(1)}, u32[]{:S(2)}, u32[]{:S(2)}) collective-permute-start(f32[1,32,512]{2,1,0:T(8,128)S(1)} %get-tuple-element.74), channel_id=1, source_target_pairs={{0,4},{4,8},{8,12},{12,16},{16,20},{20,24},{24,28},{1,5},{5,9},{9,... | collective-permute-start | bytes 196616 | tf_op jit(solution)/shard_map/ppermute | solution.py:16
  67.5 37.0 %collective-permute-start.12 = (f32[1,32,512]{2,1,0:T(8,128)S(1)}, f32[1,32,512]{2,1,0:T(8,128)S(1)}, u32[]{:S(2)}, u32[]{:S(2)}) collective-permute-start(f32[1,32,512]{2,1,0:T(8,128)S(1)} %get-tuple-element.75), channel_id=1, source_target_pairs={{4,0},{8,4},{12,8},{16,12},{20,16},{24,20},{28,24},{5,1},{9,5},{13... | collective-permute-start | bytes 196616 | tf_op jit(solution)/shard_map/ppermute | solution.py:19
  68.9 40.1 %collective-permute-start.14 = (f32[1,32,512]{2,1,0:T(8,128)S(1)}, f32[1,32,512]{2,1,0:T(8,128)S(1)}, u32[]{:S(2)}, u32[]{:S(2)}) collective-permute-start(f32[1,32,512]{2,1,0:T(8,128)S(1)} %get-tuple-element.76), channel_id=1, source_target_pairs={{1,0},{2,1},{3,2},{5,4},{6,5},{7,6},{9,8},{10,9},{11,10},{13,12},{... | collective-permute-start | bytes 196616 | tf_op jit(solution)/shard_map/ppermute | solution.py:19
  70.3 40.3 %collective-permute-start.13 = (f32[1,32,512]{2,1,0:T(8,128)S(1)}, f32[1,32,512]{2,1,0:T(8,128)S(1)}, u32[]{:S(2)}, u32[]{:S(2)}) collective-permute-start(f32[1,32,512]{2,1,0:T(8,128)S(1)} %get-tuple-element.77), channel_id=1, source_target_pairs={{0,1},{1,2},{2,3},{4,5},{5,6},{6,7},{8,9},{9,10},{10,11},{12,13},{... | collective-permute-start | bytes 196616 | tf_op jit(solution)/shard_map/ppermute | solution.py:16
  99.5 11.1 %collective-permute-start.7 = (f32[1,32,512]{2,1,0:T(8,128)S(1)}, f32[1,32,512]{2,1,0:T(8,128)S(1)}, u32[]{:S(2)}, u32[]{:S(2)}) collective-permute-start(f32[1,32,512]{2,1,0:T(8,128)S(1)} %get-tuple-element.78), channel_id=1, source_target_pairs={{0,4},{4,8},{8,12},{12,16},{16,20},{20,24},{24,28},{1,5},{5,9},{9,... | collective-permute-start | bytes 196616 | tf_op jit(solution)/shard_map/ppermute | solution.py:16
  103.2 7.4 collective-permute-start.10
  104.5 6.4 collective-permute-start.9
  109.1 4.4 collective-permute-start.8
  118.0 5.9 collective-permute-start.16
  144.8 8.5 collective-permute-start.18
  146.1 7.2 collective-permute-start.21
  147.4 6.4 collective-permute-start.20
  152.0 4.8 collective-permute-start.19
  244.4 8.5 collective-permute-start.22
  245.7 7.2 collective-permute-start.25
  247.0 6.4 collective-permute-start.24
  251.6 5.2 collective-permute-start.23
  261.3 4.1 collective-permute-start.27
  287.7 8.6 collective-permute-start.29
  289.0 7.3 collective-permute-start.32
  290.3 6.4 collective-permute-start.31
  294.9 4.9 collective-permute-start.30
  386.8 8.5 collective-permute-start.33
  388.1 7.2 collective-permute-start.36
  389.4 6.4 collective-permute-start.35
  394.0 5.2 collective-permute-start.34
  403.7 4.1 collective-permute-start.38
  430.1 8.9 collective-permute-start.40
  431.4 7.6 collective-permute-start.43
  432.7 6.4 collective-permute-start.42
  437.3 4.8 collective-permute-start.41
  529.5 8.5 collective-permute-start.44
  530.8 7.2 collective-permute-start.47
  532.1 6.4 collective-permute-start.46
  536.7 5.2 collective-permute-start.45
  546.4 4.1 collective-permute-start.49
  572.8 8.7 collective-permute-start.51
  574.1 7.4 collective-permute-start.54
  575.4 6.4 collective-permute-start.53
  580.0 4.8 collective-permute-start.52
  672.1 8.5 collective-permute-start.55
  673.4 7.2 collective-permute-start.58
  674.7 6.4 collective-permute-start.57
  679.3 5.2 collective-permute-start.56
  689.0 4.1 collective-permute-start.60
  715.4 8.6 collective-permute-start.62
  716.7 7.3 collective-permute-start.65
  718.0 6.4 collective-permute-start.64
  722.6 4.8 collective-permute-start.63
  814.8 8.5 collective-permute-start.66
  816.1 7.2 collective-permute-start.69
  817.4 6.4 collective-permute-start.68
  822.0 5.2 collective-permute-start.67
  831.7 4.1 collective-permute-start.71
  858.1 8.7 collective-permute-start.73
  859.4 7.4 collective-permute-start.76
  860.7 6.4 collective-permute-start.75
  865.3 4.9 collective-permute-start.74
  (18 other events, 307.1 us)
